TPU v7x, 256 devices: a whole 4x4x8 slice. The times are simulated.
256 devices in a mesh: rows: 64 (over z, y, core), cols: 4 (over x).
Axes of the slice: x: 4, y: 4, z: 8, core: 2. Of those that a mesh axis runs over, the one named last changes fastest.
Arguments:
- feats_t: bfloat16 [128, 131072], P('cols', 'rows'), may hold values from -6 to 6
- adj_index: int32 [1024, 16], replicated, may hold values from 0 to 1023, as said below
- adj_weight: bfloat16 [1024, 16, 128, 128], P('rows'), as said below
- weight: bfloat16 [128, 256], replicated, may hold values from -0.5 to 0.5
- cotangent_t: bfloat16 [256, 131072], P('cols', 'rows'), may hold values from -6 to 6
Outputs:
- output_t: bfloat16 [256, 131072], P('cols', 'rows')
- weight_grad: float32 [128, 256], P('cols')
- feat_grad: float32 [128, 131072], P('cols', 'rows')
Inputs may be any that keep to these rules, and one draw needn't show every extreme that they name: `adj_index`: slot 0 of row block i names block i itself. Blocks are grouped 16 to a device in order. Slot 1 names a block of the next device (device index plus one, cyclically). The row blocks of one device name at most 4 distinct blocks of any other device, and exactly 4 of the next one. A block may stand in several slots of one row block. `adj_weight`: Nonnegative; about one entry in eight is nonzero.
All inputs are finite; a program needn't handle non-finite values.
Results may differ from a plain program's by a relative error of at most 0.0054.
Values may be sent and summed in bfloat16 or wider, within the bound.
A program may use at most 128 MiB of HBM per device.

v0:
```python
import math
import jax
import jax.numpy as jnp
from jax import lax
from jax.sharding import PartitionSpec as P


def body(feats_t, adj_index, adj_weight, weight, cotangent_t):
    feat_rows, node_cols = feats_t.shape
    blocks_n = adj_weight.shape[0]
    slots_n = adj_weight.shape[1]
    tile_n = adj_weight.shape[2]
    row_devs = lax.axis_size("rows")
    row_pos = lax.axis_index("rows")
    col_pos = lax.axis_index("cols")
    unit_rows = cotangent_t.shape[0]
    own_index = lax.dynamic_slice_in_dim(adj_index, row_pos * blocks_n, blocks_n, 0)
    own_flat = own_index.reshape(-1)
    local_tiles = feats_t.reshape(feat_rows, blocks_n, tile_n).transpose(1, 0, 2)
    whole_panel = lax.all_gather(local_tiles, "rows", axis=0, tiled=True)
    picked = whole_panel[own_index]
    aggregate = jnp.einsum("bkfj,bkij->fbi", picked, adj_weight, preferred_element_type=jnp.float32)
    aggregated = aggregate.reshape(feat_rows, node_cols).astype(jnp.bfloat16)
    w_slab = lax.dynamic_slice_in_dim(weight, col_pos * unit_rows, unit_rows, 1)
    pre_act = lax.dot_general(
        w_slab,
        lax.all_gather(aggregated, "cols", axis=0, tiled=True),
        (((0,), (0,)), ((), ())),
        preferred_element_type=jnp.float32,
    )
    output_t = jax.nn.silu(pre_act).astype(jnp.bfloat16)
    sigm = jax.nn.sigmoid(pre_act)
    pre_grad = (cotangent_t.astype(jnp.float32) * sigm * (1.0 + pre_act * (1.0 - sigm))).astype(
        jnp.bfloat16
    )
    w_mine = lax.dynamic_slice_in_dim(weight, col_pos * feat_rows, feat_rows, 0)
    portion = lax.all_gather(pre_grad, "cols", axis=0, tiled=True)
    grad_acc = jnp.dot(w_mine, portion, preferred_element_type=jnp.float32)
    block_grad = lax.dot_general(
        aggregated, portion, (((1,), (1,)), ((), ())), preferred_element_type=jnp.float32
    )
    grad_scale = 1.0 / math.sqrt(node_cols * row_devs)
    weight_grad = lax.psum(block_grad, "rows") * grad_scale
    agg_grad = grad_acc.astype(jnp.bfloat16)
    contrib = jnp.einsum(
        "fbi,bkij->bkfj",
        agg_grad.reshape(feat_rows, blocks_n, tile_n),
        adj_weight,
        preferred_element_type=jnp.float32,
    )
    contrib_flat = contrib.reshape(blocks_n * slots_n, feat_rows * tile_n)
    buffer = jax.ops.segment_sum(contrib_flat, own_flat, num_segments=row_devs * blocks_n)
    buffer = buffer.reshape(row_devs * blocks_n, feat_rows, tile_n)
    summed = lax.psum_scatter(buffer, "rows", scatter_dimension=0, tiled=True)
    feat_grad = summed.transpose(1, 0, 2).reshape(feat_rows, node_cols)
    return (output_t, weight_grad, feat_grad)


def solution(mesh):
    return jax.shard_map(
        body,
        mesh=mesh,
        in_specs=(P("cols", "rows"), P(), P("rows", None, None, None), P(), P("cols", "rows")),
        out_specs=(P("cols", "rows"), P("cols", None), P("cols", "rows")),
        check_vma=False,
    )
```

profile of v0, /device:TPU:4, one launch (start us, length us, event | category | flops | bytes accessed | tf_op | source)
XLA Modules:
  0.0 468.2 jit_solution(11323263088289372892)
XLA Ops:
  7.2 0.0 copy-start
  7.2 0.0 copy-start.3
  7.2 0.0 all-gather.3.cloned.1.call-start
  7.2 1.0 copy.36
  8.2 0.7 copy.22
  8.9 0.0 all-gather.3.cloned.1.call-update
  8.9 0.0 all-gather.5.cloned.1.call-start
  9.0 0.8 compare_select_fusion
  9.8 0.1 copy.23
  9.8 0.1 reshape.30
  9.9 87.4 %all-gather.3.cloned.1.call-done = bf16[1024,32,128]{2,1,0:T(8,128)(2,1)} async-done(((bf16[16,32,128]{2,1,0:T(8,128)(2,1)}), bf16[1024,32,128]{2,1,0:T(8,128)(2,1)}) %all-gather.3.cloned.1.call-update) | async-done | bytes 8388624 | tf_op jit(solution)/shard_map/all_gather | solution.py:20
  97.4 4.4 gather_fusion
  101.7 6.2 %fusion.5 = bf16[16,4,8,128]{3,2,1,0:T(8,128)(2,1)S(1)} fusion(bf16[16,16,32,128]{3,2,1,0:T(8,128)(2,1)S(1)} %bitcast.45, bf16[16,16,128,128]{3,2,1,0:T(8,128)(2,1)} %param.7), kind=kOutput, calls=%fused_computation.9 | convolution fusion | flops 268500992 | bytes 10616832 | tf_op jit(solution)/shard_map/bkfj,bkij->fbi/dot_general | solution.py:22
  108.0 11.6 %all_gather.10 = bf16[128,2048]{1,0:T(8,128)(2,1)S(1)} all-gather(bf16[32,2048]{1,0:T(8,128)(2,1)S(1)} %bitcast.47), channel_id=1, replica_groups=mesh['rows'=64,'cols'=4] {'cols'}, dimensions={0}, use_global_device_ids=true | all-gather | bytes 655360 | tf_op jit(solution)/shard_map/all_gather | solution.py:27
  119.5 0.0 copy-done
  119.5 0.0 copy-done.3
  119.5 1.3 multiply_convert_fusion
  120.8 0.0 all-gather.5.cloned.1.call-update
  120.9 0.2 reduce-scatter.2.cloned.1.call-start
  121.1 0.1 copy.25
  121.2 0.1 reshape.38
  121.3 24.2 %all-gather.5.cloned.1.call-done = bf16[256,2048]{1,0:T(8,128)(2,1)} async-done(((bf16[64,2048]{1,0:T(8,128)(2,1)}), bf16[256,2048]{1,0:T(8,128)(2,1)}) %all-gather.5.cloned.1.call-update) | async-done | bytes 1048592 | tf_op jit(solution)/shard_map/all_gather | solution.py:37
  145.5 1.5 fusion.6
  147.0 6.5 %fusion.7 = f32[16,32,16,128]{3,1,2,0:T(8,128)} fusion(bf16[16,16,128,128]{3,2,1,0:T(8,128)(2,1)} %param.7, bf16[32,16,128,1]{2,1,0,3:T(8,128)(2,1)S(1)} %bitcast.46), kind=kOutput, calls=%fused_computation.16 | convolution fusion | flops 268435456 | bytes 12713984 | tf_op jit(solution)/shard_map/fbi,bkij->bkfj/dot_general | solution.py:45
  153.6 16.7 %scatter_custom_fusion = f32[1024,4096]{1,0:T(8,128)} fusion(s32[256]{0:T(256)S(1)} %reshape.38, f32[]{:T(128)} %constant.11.clone.1, f32[32,8,32,128]{3,2,1,0:T(8,128)} %bitcast.44), kind=kCustom, calls=%fused_computation.2 | custom fusion | flops 1048576 | bytes 20971524 | tf_op jit(solution)/shard_map/scatter-add | solution.py:52
  170.3 17.5 %copy.27 = f32[1024,4096]{0,1:T(8,128)} copy(f32[1024,4096]{1,0:T(8,128)} %scatter_custom_fusion) | data formatting | bytes 33554432 | tf_op jit(solution)/shard_map/scatter-add | solution.py:52
  187.7 17.4 %copy.28 = f32[1024,32,128]{2,1,0:T(8,128)} copy(f32[1024,32,128]{0,2,1:T(8,128)} %bitcast.43) | data formatting | bytes 33554432 | tf_op jit(solution)/shard_map/reshape | solution.py:53
  205.1 0.0 copy-start.1
  205.1 0.0 copy-start.2
  205.1 0.0 reduce-scatter.2.cloned.1.call-update
  205.2 1.2 copy-done.2
  206.4 0.4 fusion.14
  206.8 252.5 %psum.7 = f32[32,256]{1,0:T(8,128)S(1)} all-reduce(f32[32,256]{1,0:T(8,128)S(1)} %fusion.14), channel_id=1, replica_groups=mesh['rows'=64,'cols'=4] {'rows'}, use_global_device_ids=true, to_apply=%region_0.1 | all-reduce | flops 8192 | bytes 65536 | tf_op jit(solution)/shard_map/psum | solution.py:43
  459.4 0.6 broadcast_multiply_fusion
  460.0 0.0 reduce-scatter.2.cloned.1.call-done
  460.0 1.7 copy_bitcast_fusion
  461.6 0.0 copy-done.1
  (3 shorter events, 0.1 us)
Async XLA Ops:
  7.2 112.4 %copy-start = (bf16[128,256]{1,0:T(8,128)(2,1)S(1)}, bf16[128,256]{1,0:T(8,128)(2,1)}, u32[]{:S(2)}) copy-start(bf16[128,256]{1,0:T(8,128)(2,1)} %param.8) | copy-start | bytes 196612
  7.2 112.4 %copy-start.3 = (bf16[64,2048]{1,0:T(8,128)(2,1)S(1)}, bf16[64,2048]{1,0:T(8,128)(2,1)}, u32[]{:S(2)}) copy-start(bf16[64,2048]{1,0:T(8,128)(2,1)} %param.9) | copy-start | bytes 786436
  7.2 90.2 %all-gather.3.cloned.1.call-start = ((), (), s32[]{:S(2)}) async-start(), calls=%async_computation.1 | async-start | bytes 8519680 | tf_op jit(solution)/shard_map/all_gather | solution.py:20
  8.9 136.6 %all-gather.5.cloned.1.call-start = ((), (), s32[]{:S(2)}) async-start(), calls=%async_computation.2 | async-start | bytes 1310720 | tf_op jit(solution)/shard_map/all_gather | solution.py:37
  120.9 339.1 %reduce-scatter.2.cloned.1.call-start = ((), (), s32[]{:S(2)}) async-start(), calls=%async_computation.3 | async-start | bytes 17039360 | tf_op jit(solution)/shard_map/reduce_scatter | solution.py:54
  205.1 256.5 %copy-start.1 = (bf16[128,256]{1,0:T(8,128)(2,1)S(1)}, bf16[128,256]{1,0:T(8,128)(2,1)}, u32[]{:S(2)}) copy-start(bf16[128,256]{1,0:T(8,128)(2,1)} %param.8) | copy-start | bytes 196612
  205.1 1.3 copy-start.2
Sparse Core Ops, SparseCore 0:
  11.4 85.9 all-gather.2
  121.0 24.4 all-gather.4
  205.3 191.1 reduce-scatter.1
where the time goes:
time: 469 us; the launch traced here: 468 us
  blocking collectives  264 us (56%)
  waiting for transfers between devices  112 us (24%)
  local copies, waits for them, and re-layouts  44.2 us (9%)
  other arithmetic  18.1 us (4%)
  matrix products  15.9 us (3%)
  between operations  13.8 us (3%)
    psum x1, blocking collectives, body(): weight_grad = lax.psum(block_grad, 'rows') * grad_scale  253 us
    all_gather x1, waiting for transfers between devices, body(): whole_panel = lax.all_gather(local_tiles, 'rows', axis=0, tiled=True)  87.4 us
    all_gather x1, waiting for transfers between devices, body(): portion = lax.all_gather(pre_grad, 'cols', axis=0, tiled=True)  24.2 us
    scatter-add x1, local copies, waits for them, and re-layouts, body(): jax.ops.segment_sum(contrib_flat, own_flat, num_segments=row_devs * block...  17.5 us
    reshape x1, local copies, waits for them, and re-layouts, body(): buffer = buffer.reshape(row_devs * blocks_n, feat_rows, tile_n)  17.4 us
    scatter-add x1, other arithmetic, body(): jax.ops.segment_sum(contrib_flat, own_flat, num_segments=row_devs * block...  16.7 us
    all_gather x1, blocking collectives, body(): lax.all_gather(aggregated, 'cols', axis=0, tiled=True)  11.6 us
  transfers between devices with their start and end apart: 3, of which 2 were waited for; matrix products, arithmetic and copies ran while one was open for 0% of the time, Pallas kernels for 0%

commit v1 on v0

--- a/solution.py
+++ b/solution.py
@@ -17,7 +17,9 @@
     own_index = lax.dynamic_slice_in_dim(adj_index, row_pos * blocks_n, blocks_n, 0)
     own_flat = own_index.reshape(-1)
     local_tiles = feats_t.reshape(feat_rows, blocks_n, tile_n).transpose(1, 0, 2)
-    whole_panel = lax.all_gather(local_tiles, "rows", axis=0, tiled=True)
+    whole_panel = jnp.concatenate(
+        lax.all_to_all(jnp.stack([local_tiles] * lax.axis_size("rows")), "rows", 0, 0), axis=0
+    )
     picked = whole_panel[own_index]
     aggregate = jnp.einsum("bkfj,bkij->fbi", picked, adj_weight, preferred_element_type=jnp.float32)
     aggregated = aggregate.reshape(feat_rows, node_cols).astype(jnp.bfloat16)

time: 469 us -> 584 us (1.25)
  waiting for transfers between devices: 112 us -> 209 us
  starting transfers between devices: 0.3 us -> 12.6 us
    all_to_all x0 -> x1, waiting for transfers between devices: none -> 185 us  [body(): lax.all_to_all(jnp.stack([local_tiles] * lax.axis_size('rows')), 'rows',...]
    all_gather x1 -> x0, waiting for transfers between devices: 87.4 us -> none  [body(): whole_panel = lax.all_gather(local_tiles, 'rows', axis=0, tiled=True)]
    all_to_all x0 -> x1, starting transfers between devices: none -> 12.4 us  [body(): lax.all_to_all(jnp.stack([local_tiles] * lax.axis_size('rows')), 'rows',...]
where the time goes in v1:
time: 584 us; the launch traced here: 583 us
  blocking collectives  265 us (45%)
  waiting for transfers between devices  209 us (36%)
  local copies, waits for them, and re-layouts  48.8 us (8%)
  other arithmetic  18.1 us (3%)
  matrix products  15.9 us (3%)
  between operations  14.1 us (2%)
  starting transfers between devices  12.6 us (2%)
    psum x1, blocking collectives, body(): weight_grad = lax.psum(block_grad, 'rows') * grad_scale  253 us
    all_to_all x1, waiting for transfers between devices, body(): lax.all_to_all(jnp.stack([local_tiles] * lax.axis_size('rows')), 'rows',...  185 us
    all_gather x1, waiting for transfers between devices, body(): portion = lax.all_gather(pre_grad, 'cols', axis=0, tiled=True)  23.6 us
    scatter-add x1, local copies, waits for them, and re-layouts, body(): jax.ops.segment_sum(contrib_flat, own_flat, num_segments=row_devs * block...  17.5 us
    reshape x1, local copies, waits for them, and re-layouts, body(): buffer = buffer.reshape(row_devs * blocks_n, feat_rows, tile_n)  17.4 us
    scatter-add x1, other arithmetic, body(): jax.ops.segment_sum(contrib_flat, own_flat, num_segments=row_devs * block...  16.7 us
    all_to_all x1, starting transfers between devices, body(): lax.all_to_all(jnp.stack([local_tiles] * lax.axis_size('rows')), 'rows',...  12.4 us
    all_gather x1, blocking collectives, body(): lax.all_gather(aggregated, 'cols', axis=0, tiled=True)  12 us
  transfers between devices with their start and end apart: 3, of which 2 were waited for; matrix products, arithmetic and copies ran while one was open for 0% of the time, Pallas kernels for 0%

profile of v1, /device:TPU:4, one launch (start us, length us, event | category | flops | bytes accessed | tf_op | source)
XLA Modules:
  0.0 582.8 jit_solution(2732226325612892170)
XLA Ops:
  7.2 0.0 copy-start
  7.2 1.0 copy.37
  8.2 5.2 stack.2
  13.4 12.4 %all-to-all-start = ((bf16[64,16,32,128]{3,2,1,0:T(8,128)(2,1)}), bf16[64,16,32,128]{3,2,1,0:T(8,128)(2,1)}, u32[]{:S(2)}, u32[]{:S(2)}) async-start(bf16[64,16,32,128]{3,2,1,0:T(8,128)(2,1)} %stack.2), calls=%async_computation | async-start | bytes 16777216 | tf_op jit(solution)/shard_map/all_to_all | solution.py:21
  25.8 0.0 copy-start.3
  25.8 0.0 all-gather.2.cloned.1.call-start
  25.9 0.8 compare_select_fusion
  26.7 0.1 copy.24
  26.7 0.1 reshape.36
  26.8 185.0 %all-to-all-done = bf16[64,16,32,128]{3,2,1,0:T(8,128)(2,1)} async-done(((bf16[64,16,32,128]{3,2,1,0:T(8,128)(2,1)}), bf16[64,16,32,128]{3,2,1,0:T(8,128)(2,1)}, u32[]{:S(2)}, u32[]{:S(2)}) %all-to-all-start) | async-done | bytes 8388640 | tf_op jit(solution)/shard_map/all_to_all | solution.py:21
  211.9 4.4 gather_fusion
  216.2 6.2 %fusion.5 = bf16[16,4,8,128]{3,2,1,0:T(8,128)(2,1)S(1)} fusion(bf16[16,16,32,128]{3,2,1,0:T(8,128)(2,1)S(1)} %bitcast.46, bf16[16,16,128,128]{3,2,1,0:T(8,128)(2,1)} %param.7), kind=kOutput, calls=%fused_computation.9 | convolution fusion | flops 268500992 | bytes 10616832 | tf_op jit(solution)/shard_map/bkfj,bkij->fbi/dot_general | solution.py:24
  222.5 12.0 %all_gather.6 = bf16[128,2048]{1,0:T(8,128)(2,1)S(1)} all-gather(bf16[32,2048]{1,0:T(8,128)(2,1)S(1)} %bitcast.48), channel_id=1, replica_groups=mesh['rows'=64,'cols'=4] {'cols'}, dimensions={0}, use_global_device_ids=true | all-gather | bytes 655360 | tf_op jit(solution)/shard_map/all_gather | solution.py:29
  234.5 0.0 copy-done
  234.5 0.0 copy-done.3
  234.5 1.3 multiply_convert_fusion
  235.8 0.0 all-gather.2.cloned.1.call-update
  235.8 0.2 reduce-scatter.2.cloned.1.call-start
  236.0 0.1 copy.26
  236.1 0.1 reshape.44
  236.2 23.6 %all-gather.2.cloned.1.call-done = bf16[256,2048]{1,0:T(8,128)(2,1)} async-done(((bf16[64,2048]{1,0:T(8,128)(2,1)}), bf16[256,2048]{1,0:T(8,128)(2,1)}) %all-gather.2.cloned.1.call-update) | async-done | bytes 1048592 | tf_op jit(solution)/shard_map/all_gather | solution.py:39
  259.8 1.5 fusion.6
  261.4 6.5 %fusion.7 = f32[16,32,16,128]{3,1,2,0:T(8,128)} fusion(bf16[16,16,128,128]{3,2,1,0:T(8,128)(2,1)} %param.7, bf16[32,16,128,1]{2,1,0,3:T(8,128)(2,1)S(1)} %bitcast.47), kind=kOutput, calls=%fused_computation.16 | convolution fusion | flops 268435456 | bytes 12713984 | tf_op jit(solution)/shard_map/fbi,bkij->bkfj/dot_general | solution.py:47
  267.9 16.7 %scatter_custom_fusion = f32[1024,4096]{1,0:T(8,128)} fusion(s32[256]{0:T(256)S(1)} %reshape.44, f32[]{:T(128)} %constant.11.clone.1, f32[32,8,32,128]{3,2,1,0:T(8,128)} %bitcast.45), kind=kCustom, calls=%fused_computation.2 | custom fusion | flops 1048576 | bytes 20971524 | tf_op jit(solution)/shard_map/scatter-add | solution.py:54
  284.6 17.5 %copy.28 = f32[1024,4096]{0,1:T(8,128)} copy(f32[1024,4096]{1,0:T(8,128)} %scatter_custom_fusion) | data formatting | bytes 33554432 | tf_op jit(solution)/shard_map/scatter-add | solution.py:54
  302.0 17.4 %copy.29 = f32[1024,32,128]{2,1,0:T(8,128)} copy(f32[1024,32,128]{0,2,1:T(8,128)} %bitcast.44) | data formatting | bytes 33554432 | tf_op jit(solution)/shard_map/reshape | solution.py:55
  319.4 0.0 copy-start.1
  319.4 0.0 copy-start.2
  319.4 0.0 reduce-scatter.2.cloned.1.call-update
  319.5 1.2 copy-done.2
  320.7 0.4 fusion.14
  321.1 252.5 %psum.7 = f32[32,256]{1,0:T(8,128)S(1)} all-reduce(f32[32,256]{1,0:T(8,128)S(1)} %fusion.14), channel_id=1, replica_groups=mesh['rows'=64,'cols'=4] {'rows'}, use_global_device_ids=true, to_apply=%region_0.1 | all-reduce | flops 8192 | bytes 65536 | tf_op jit(solution)/shard_map/psum | solution.py:45
  573.6 0.6 broadcast_multiply_fusion
  574.2 0.0 reduce-scatter.2.cloned.1.call-done
  574.2 1.7 copy_bitcast_fusion
  575.9 0.0 copy-done.1
  (4 shorter events, 0.1 us)
Async XLA Ops:
  7.2 227.3 %copy-start = (bf16[128,256]{1,0:T(8,128)(2,1)S(1)}, bf16[128,256]{1,0:T(8,128)(2,1)}, u32[]{:S(2)}) copy-start(bf16[128,256]{1,0:T(8,128)(2,1)} %param.8) | copy-start | bytes 196612
  13.4 198.4 %all-to-all-start = ((bf16[64,16,32,128]{3,2,1,0:T(8,128)(2,1)}), bf16[64,16,32,128]{3,2,1,0:T(8,128)(2,1)}, u32[]{:S(2)}, u32[]{:S(2)}) async-start(bf16[64,16,32,128]{3,2,1,0:T(8,128)(2,1)} %stack.2), calls=%async_computation | async-start | bytes 16777216 | tf_op jit(solution)/shard_map/all_to_all | solution.py:21
  25.8 208.7 %copy-start.3 = (bf16[64,2048]{1,0:T(8,128)(2,1)S(1)}, bf16[64,2048]{1,0:T(8,128)(2,1)}, u32[]{:S(2)}) copy-start(bf16[64,2048]{1,0:T(8,128)(2,1)} %param.9) | copy-start | bytes 786436
  25.8 234.0 %all-gather.2.cloned.1.call-start = ((), (), s32[]{:S(2)}) async-start(), calls=%async_computation.2 | async-start | bytes 1310720 | tf_op jit(solution)/shard_map/all_gather | solution.py:39
  235.8 338.4 %reduce-scatter.2.cloned.1.call-start = ((), (), s32[]{:S(2)}) async-start(), calls=%async_computation.3 | async-start | bytes 17039360 | tf_op jit(solution)/shard_map/reduce_scatter | solution.py:56
  319.4 256.5 %copy-start.1 = (bf16[128,256]{1,0:T(8,128)(2,1)S(1)}, bf16[128,256]{1,0:T(8,128)(2,1)}, u32[]{:S(2)}) copy-start(bf16[128,256]{1,0:T(8,128)(2,1)} %param.8) | copy-start | bytes 196612
  319.4 1.3 copy-start.2
Sparse Core Ops, SparseCore 0:
  235.9 23.8 all-gather.1
  319.6 191.1 reduce-scatter.1
